TPU v7x, 32 devices: a whole 2x2x4 slice. The times are simulated.
32 devices in a mesh: req: 4 (over y, x), tp: 2 (over core), kv: 4 (over z).
Axes of the slice: x: 2, y: 2, z: 4, core: 2. Of those that a mesh axis runs over, the one named last changes fastest.
Arguments:
- hidden_in: bfloat16 [4, 512, 7168], P('req', 'tp', 'kv'), may hold values from -6 to 6
- lengths: int32 [4], P('req'), may hold values from 96 to 1536, as said below
- ln_gain: bfloat16 [7168], P('kv'), may hold values from 0.099609375 to 1.8984375
- ln_bias: bfloat16 [7168], P('kv'), may hold values from -3 to 3
- w_qkv: bfloat16 [7168, 768], P('kv', 'tp'), may hold values from -0.0625 to 0.0625
- qkv_bias: bfloat16 [768], P('tp'), may hold values from -3 to 3
- cache_keys: bfloat16 [4, 2, 1536, 128], P('req', 'tp', 'kv')
- cache_values: bfloat16 [4, 2, 1536, 128], P('req', 'tp', 'kv'), may hold values from -6 to 6
- w_out: bfloat16 [256, 7168], P('tp', 'kv'), may hold values from -0.375 to 0.375
- out_bias: bfloat16 [7168], P('kv'), may hold values from -3 to 3
Outputs:
- hidden_out: bfloat16 [4, 512, 7168], P('req', 'tp', 'kv')
- new_keys: bfloat16 [4, 2, 512, 128], P('req', 'tp', 'kv')
- new_values: bfloat16 [4, 2, 512, 128], P('req', 'tp', 'kv')
Inputs may be any that keep to these rules, and one draw needn't show every extreme that they name: Request r's cache holds keys and values at its first lengths[r] positions; some request's cache is full in every draw.
All inputs are finite; a program needn't handle non-finite values.
Results may differ from a plain program's by a relative error of at most 0.012.
The roundings to bfloat16 on the way count: a program that leaves them out, or rounds other values in their place, can miss the bound.
Values may be sent and summed in bfloat16 or wider, within the bound.
A program may use at most 64 MiB of HBM per device.

v0:
```python
import jax
import jax.numpy as jnp
from jax import lax
from jax.sharding import PartitionSpec as P

D = 7168


epsilon = 1e-05
neg_large = -1e30


def update_state(state, scores, visible, value_rows):
    row_max, row_sum, weighted = state
    scores = jnp.where(visible, scores, neg_large)
    max_next = jnp.maximum(row_max, jnp.max(scores, axis=1))
    weights = jnp.where(visible, jnp.exp(scores - max_next[:, None]), 0.0)
    rescale = jnp.exp(row_max - max_next)
    sum_next = row_sum * rescale + jnp.sum(weights, axis=1)
    mixed = jnp.dot(weights.astype(jnp.bfloat16), value_rows, preferred_element_type=jnp.float32)
    return (max_next, sum_next, weighted * rescale[:, None] + mixed)


def on_device(
    hidden_in, lengths, ln_gain, ln_bias, w_qkv, qkv_bias, cache_keys, cache_values, w_out, out_bias
):
    rows = hidden_in[0].astype(jnp.float32)
    sums, squares = lax.psum((jnp.sum(rows, axis=1), jnp.sum(rows * rows, axis=1)), "kv")
    row_mean = sums / D
    row_var = squares / D - row_mean * row_mean
    normed = (
        (rows - row_mean[:, None])
        * lax.rsqrt(row_var + epsilon)[:, None]
        * ln_gain.astype(jnp.float32)
        + ln_bias.astype(jnp.float32)
    ).astype(jnp.bfloat16)
    partial_value = jnp.dot(
        lax.all_gather(normed, "tp", axis=0, tiled=True), w_qkv, preferred_element_type=jnp.float32
    )
    summed = lax.psum(partial_value, "kv")
    projected = (summed + qkv_bias.astype(jnp.float32)).astype(jnp.bfloat16)
    head_size = cache_keys.shape[3]
    queries = projected[:, :head_size]
    keys_new = projected[:, head_size : 2 * head_size]
    values_new = projected[:, 2 * head_size :]
    group_len = queries.shape[0]
    kv_index = lax.axis_index("kv")
    kv_count = lax.axis_size("kv")
    part_len = cache_keys.shape[2]
    keys_old = cache_keys[0, 0]
    values_old = cache_values[0, 0]
    length = lengths[0]
    score_scale = head_size ** (-0.5)
    block_len = min(1024, part_len)

    def block_step(block, state):
        offset = block * block_len
        scores = jnp.dot(queries, keys_old.T, preferred_element_type=jnp.float32) * score_scale
        positions = kv_index * part_len + offset + jnp.arange(block_len, dtype=jnp.int32)
        visible = jnp.broadcast_to((positions < length)[None, :], scores.shape)
        return update_state(state, scores, visible, values_old)

    state = (
        jnp.full((group_len,), neg_large, jnp.float32),
        jnp.zeros((group_len,), jnp.float32),
        jnp.zeros((group_len, head_size), jnp.float32),
    )
    state = lax.fori_loop(0, part_len // block_len, block_step, state)
    own_len = group_len // kv_count
    own_start = kv_index * own_len
    own_keys = lax.dynamic_slice_in_dim(keys_new, own_start, own_len, 0)
    own_values = lax.dynamic_slice_in_dim(values_new, own_start, own_len, 0)
    group_scores = jnp.dot(queries, own_keys.T, preferred_element_type=jnp.float32) * score_scale
    key_index = own_start + jnp.arange(own_len, dtype=jnp.int32)
    query_index = jnp.arange(group_len, dtype=jnp.int32)
    causal = key_index[None, :] <= query_index[:, None]
    state = update_state(state, group_scores, causal, own_values)
    row_max, row_sum, weighted = state
    global_max = lax.pmax(row_max, "kv")
    factor = jnp.exp(row_max - global_max)
    row_sum, weighted = (
        lax.psum((row_sum * factor).astype(jnp.bfloat16), "kv").astype(jnp.float32),
        lax.psum((weighted * factor[:, None]).astype(jnp.bfloat16), "kv").astype(jnp.float32),
    )
    attended = (weighted / row_sum[:, None]).astype(jnp.bfloat16)
    head_total = lax.psum_scatter(
        jnp.dot(attended, w_out, preferred_element_type=jnp.float32).astype(jnp.bfloat16),
        "tp",
        scatter_dimension=0,
        tiled=True,
    ).astype(jnp.float32)
    hidden_out = (head_total + out_bias.astype(jnp.float32) + rows).astype(jnp.bfloat16)[None]
    return (hidden_out, own_keys[None, None], own_values[None, None])


def solution(mesh):
    placed = (
        P("req", "tp", "kv"),
        P("req"),
        P("kv"),
        P("kv"),
        P("kv", "tp"),
        P("tp"),
        P("req", "tp", "kv", None),
        P("req", "tp", "kv", None),
        P("tp", "kv"),
        P("kv"),
    )
    return jax.shard_map(
        on_device,
        mesh=mesh,
        in_specs=placed,
        out_specs=(P("req", "tp", "kv"), P("req", "tp", "kv", None), P("req", "tp", "kv", None)),
        check_vma=False,
    )
```

profile of v0, /device:TPU:1, one launch (start us, length us, event | category | flops | bytes accessed | tf_op | source)
XLA Modules:
  0.0 150.3 jit_solution(10269492212784642391)
XLA Ops:
  7.2 0.0 copy-start
  7.2 0.0 copy-start.1
  7.2 0.0 all-gather.2.cloned.1.call-start
  7.3 1.6 %fusion.7 = f32[256]{0:T(256)S(1)} fusion(bf16[1,256,1792]{2,1,0:T(8,128)(2,1)} %param.10), kind=kLoop, calls=%fused_computation.10 | loop fusion | flops 1376000 | bytes 918528 | tf_op jit(solution)/shard_map/reduce_sum | solution.py:28
  8.8 1.4 convert_reduce_fusion
  10.3 10.8 %all-reduce = (f32[256]{0:T(256)S(1)}, f32[256]{0:T(256)S(1)}) all-reduce(f32[256]{0:T(256)S(1)} %fusion.7, f32[256]{0:T(256)S(1)} %convert_reduce_fusion), channel_id=1, replica_groups=mesh['req'=4,'tp'=2,'kv'=4] {'kv'}, use_global_device_ids=true, to_apply=%region_3.0 | all-reduce | flops 512 | bytes 4096 | tf_op jit(solution)/shard_map/psum | solution.py:28
  21.1 1.3 fusion.6
  22.4 0.0 all-gather.2.cloned.1.call-update
  22.4 0.0 all-reduce.4.cloned.1.call-start
  22.5 10.9 %all-gather.2.cloned.1.call-done = bf16[512,1792]{1,0:T(8,128)(2,1)} async-done(((bf16[256,1792]{1,0:T(8,128)(2,1)}), bf16[512,1792]{1,0:T(8,128)(2,1)}) %all-gather.2.cloned.1.call-update) | async-done | bytes 1835024 | tf_op jit(solution)/shard_map/all_gather | solution.py:38
  33.4 3.5 %fusion.42 = f32[512,384]{1,0:T(8,128)} fusion(bf16[512,1792]{1,0:T(8,128)(2,1)} %all-gather.2.cloned.1.call-done, bf16[1792,384]{1,0:T(8,128)(2,1)S(1)} %copy-done), kind=kOutput, calls=%fused_computation.63 | convolution fusion | flops 704643072 | bytes 3997696 | tf_op jit(solution)/shard_map/dot_general | solution.py:37
  36.9 0.0 all-reduce.4.cloned.1.call-update
  36.9 0.0 all-reduce.6.cloned.1.call-start
  37.7 43.8 %all-reduce.4.cloned.1.call-done = f32[512,384]{1,0:T(8,128)} async-done(((f32[512,384]{1,0:T(8,128)}), f32[512,384]{1,0:T(8,128)}) %all-reduce.4.cloned.1.call-update) | async-done | bytes 786448 | tf_op jit(solution)/shard_map/psum | solution.py:40
  81.5 1.2 add_convert_fusion
  82.7 0.3 fusion.40
  83.0 0.2 fusion.41
  83.2 0.2 copy-done.2
  83.4 7.8 %pmax.7 = f32[512]{0:T(512)S(1)} all-reduce(f32[512]{0:T(512)S(1)} %get-tuple-element.41), channel_id=1, replica_groups=mesh['req'=4,'tp'=2,'kv'=4] {'kv'}, use_global_device_ids=true, to_apply=%region_7.0 | all-reduce | flops 512 | bytes 4096 | tf_op jit(solution)/shard_map/pmax | solution.py:79
  91.2 0.1 fusion.21
  91.3 0.2 fusion.15
  91.5 1.3 fusion.12
  92.8 1.0 fusion.13
  93.7 0.0 all-reduce.6.cloned.1.call-update
  93.8 0.0 reduce-scatter.2.cloned.1.call-start
  93.8 7.2 %psum.39 = bf16[512]{0:T(512)(128)(2,1)S(1)} all-reduce(bf16[512]{0:T(512)(128)(2,1)S(1)} %get-tuple-element.25), channel_id=1, replica_groups=mesh['req'=4,'tp'=2,'kv'=4] {'kv'}, use_global_device_ids=true, to_apply=%region_11.12 | all-reduce | flops 512 | bytes 2048 | tf_op jit(solution)/shard_map/psum | solution.py:82
  101.0 25.7 %all-reduce.6.cloned.1.call-done = bf16[512,128]{1,0:T(8,128)(2,1)} async-done(((bf16[512,128]{1,0:T(8,128)(2,1)}), bf16[512,128]{1,0:T(8,128)(2,1)}) %all-reduce.6.cloned.1.call-update) | async-done | bytes 131088 | tf_op jit(solution)/shard_map/psum | solution.py:83
  126.7 3.0 %convolution_convert_fusion = bf16[512,1792]{1,0:T(8,128)(2,1)} fusion(bf16[128,1792]{1,0:T(8,128)(2,1)} %param.18, bf16[512,128]{1,0:T(8,128)(2,1)} %all-reduce.6.cloned.1.call-done, f32[512]{0:T(512)S(1)} %convert_element_type.67), kind=kOutput, calls=%fused_computation | convolution fusion | flops 235995136 | bytes 2426880 | tf_op jit(solution)/shard_map/dot_general | solution.py:87
  129.8 0.0 reduce-scatter.2.cloned.1.call-update
  129.8 1.4 dynamic-slice_bitcast_fusion
  131.2 10.2 %reduce-scatter.2.cloned.1.call-done = bf16[256,1792]{1,0:T(8,128)(2,1)} async-done(((bf16[512,1792]{1,0:T(8,128)(2,1)}), bf16[256,1792]{1,0:T(8,128)(2,1)}) %reduce-scatter.2.cloned.1.call-update) | async-done | bytes 917520 | tf_op jit(solution)/shard_map/reduce_scatter | solution.py:86
  141.4 2.4 %fusion.14 = bf16[1,256,1792]{2,1,0:T(8,128)(2,1)} fusion(bf16[1,256,1792]{2,1,0:T(8,128)(2,1)S(1)} %copy-done.1, bf16[256,1792]{1,0:T(8,128)(2,1)} %reduce-scatter.2.cloned.1.call-done, f32[1792]{0:T(1024)S(1)} %convert_element_type.71), kind=kLoop, calls=%fused_computation.21 | loop fusion | flops 2293760 | bytes 2759680 | tf_op jit(solution)/shard_map/broadcast_in_dim | solution.py:92
  (24 shorter events, 0.1 us)
Async XLA Ops:
  7.2 26.2 %copy-start = (bf16[1792,384]{1,0:T(8,128)(2,1)S(1)}, bf16[1792,384]{1,0:T(8,128)(2,1)}, u32[]{:S(2)}) copy-start(bf16[1792,384]{1,0:T(8,128)(2,1)} %param.14) | copy-start | bytes 4128772
  7.2 13.9 %copy-start.1 = (bf16[1,256,1792]{2,1,0:T(8,128)(2,1)S(1)}, bf16[1,256,1792]{2,1,0:T(8,128)(2,1)}, u32[]{:S(2)}) copy-start(bf16[1,256,1792]{2,1,0:T(8,128)(2,1)} %param.10) | copy-start | bytes 2752516
  7.2 3.0 %copy-start.4 = (bf16[1792]{0:T(1024)(128)(2,1)S(1)}, bf16[1792]{0:T(1024)(128)(2,1)}, u32[]{:S(2)}) copy-start(bf16[1792]{0:T(1024)(128)(2,1)} %param.12) | copy-start | bytes 10756
  7.2 3.0 %copy-start.5 = (bf16[1792]{0:T(1024)(128)(2,1)S(1)}, bf16[1792]{0:T(1024)(128)(2,1)}, u32[]{:S(2)}) copy-start(bf16[1792]{0:T(1024)(128)(2,1)} %param.13) | copy-start | bytes 10756
  7.2 26.2 %all-gather.2.cloned.1.call-start = ((), (), s32[]{:S(2)}) async-start(), calls=%async_computation.1 | async-start | bytes 2752512 | tf_op jit(solution)/shard_map/all_gather | solution.py:38
  22.4 15.2 %copy-start.7 = (bf16[384]{0:T(512)(128)(2,1)S(1)}, bf16[384]{0:T(512)(128)(2,1)}, u32[]{:S(2)}) copy-start(bf16[384]{0:T(512)(128)(2,1)} %param.15) | copy-start | bytes 2308
  22.4 59.0 %all-reduce.4.cloned.1.call-start = ((), (), s32[]{:S(2)}) async-start(), calls=%async_computation.2 | async-start | bytes 1572864 | tf_op jit(solution)/shard_map/psum | solution.py:40
  36.9 45.8 %copy-start.3 = (bf16[1,1,384,128]{3,2,1,0:T(8,128)(2,1)S(1)}, bf16[1,1,384,128]{3,2,1,0:T(8,128)(2,1)}, u32[]{:S(2)}) copy-start(bf16[1,1,384,128]{3,2,1,0:T(8,128)(2,1)} %param.16) | copy-start | bytes 294916
  36.9 89.8 %all-reduce.6.cloned.1.call-start = ((), (), s32[]{:S(2)}) async-start(), calls=%async_computation.3 | async-start | bytes 262144 | tf_op jit(solution)/shard_map/psum | solution.py:83
  82.7 0.7 copy-start.2
  93.8 47.7 %reduce-scatter.2.cloned.1.call-start = ((), (), s32[]{:S(2)}) async-start(), calls=%async_computation.4 | async-start | bytes 2752512 | tf_op jit(solution)/shard_map/reduce_scatter | solution.py:86
  101.0 28.8 %copy-start.6 = (bf16[1792]{0:T(1024)(128)(2,1)S(1)}, bf16[1792]{0:T(1024)(128)(2,1)}, u32[]{:S(2)}) copy-start(bf16[1792]{0:T(1024)(128)(2,1)} %param.19) | copy-start | bytes 10756
Sparse Core Ops, SparseCore 0:
  22.5 10.8 all-gather.1
  37.0 44.3 all-reduce.3
  93.9 32.8 all-reduce.5
  129.9 11.4 reduce-scatter.1
where the time goes:
time: 151 us; the launch traced here: 150 us
  waiting for transfers between devices  90.7 us (60%)
  blocking collectives  25.8 us (17%)
  between operations  14.6 us (10%)
  matrix products  9.28 us (6%)
  other arithmetic  8.2 us (5%)
  local copies, waits for them, and re-layouts  1.61 us (1%)
    psum x1, waiting for transfers between devices, on_device(): summed = lax.psum(partial_value, 'kv')  43.8 us
    psum x1, waiting for transfers between devices, on_device(): lax.psum((weighted * factor[:, None]).astype(jnp.bfloat16), 'kv')  25.7 us
    all_gather x1, waiting for transfers between devices, on_device(): lax.all_gather(normed, 'tp', axis=0, tiled=True)  10.9 us
    psum x1, blocking collectives, on_device(): lax.psum((jnp.sum(rows, axis=1), jnp.sum(rows * rows, axis=1)), 'kv')  10.8 us
    reduce_scatter x1, waiting for transfers between devices, on_device(): lax.psum_scatter(jnp.dot(attended, w_out, preferred_element_type=jnp.floa...  10.2 us
    pmax x1, blocking collectives, on_device(): global_max = lax.pmax(row_max, 'kv')  7.82 us
    psum x1, blocking collectives, on_device(): lax.psum((row_sum * factor).astype(jnp.bfloat16), 'kv').astype(jnp.float32)  7.17 us
    dot_general x1, matrix products, on_device(): jnp.dot(lax.all_gather(normed, 'tp', axis=0, tiled=True), w_qkv, preferre...  3.49 us
  transfers between devices with their start and end apart: 4, of which 4 were waited for; matrix products, arithmetic and copies ran while one was open for 1% of the time, Pallas kernels for 0%

commit v1 on v0

v1 whole, which is shorter than its diff:
```python
import functools

import jax
import jax.numpy as jnp
from jax import lax
from jax.experimental import pallas as pl
from jax.experimental.pallas import tpu as pltpu
from jax.sharding import PartitionSpec as P

epsilon = 1e-05
neg_large = -1e30
MESH = pl.DeviceIdType.MESH
LANES = 128


def kernel(
    T, K, D,
    len_ref, x_hbm, w_hbm, keys_hbm, values_hbm, wout_hbm, params_ref, qkvb_ref,
    out_ref, nk_ref, nv_ref,
    x_v, w_v, k_v, v_v, wout_v,
    stat_out, stat_in, nrm, part, rbuf, q_buf, ot_out, ot_in, ml_out, ml_in, att_own, att_in,
    loc_sem, st_s, st_r, nm_s, nm_r, wo_s, wo_r, rs_s, rs_r, q_s, q_r, o_s, o_r, m_s, m_r, a_s, a_r,
):
    t = lax.axis_index("tp")
    z = lax.axis_index("kv")
    tok, feat = x_v.shape
    hd = k_v.shape[1]
    part_len = k_v.shape[0]
    group = T * tok
    qb = group // K
    c = min(tok, qb)
    tokp = stat_out.shape[1]

    def kv_peer(d):
        return lax.rem(z + d, K)

    def tp_peer(d):
        return lax.rem(t + d, T)

    barrier = pltpu.get_barrier_semaphore()
    for a in range(T):
        for b in range(K):
            if a or b:
                pl.semaphore_signal(barrier, inc=1, device_id={"tp": tp_peer(a), "kv": kv_peer(b)}, device_id_type=MESH)
    fetches = []
    for i, (src, dst) in enumerate(((x_hbm, x_v), (wout_hbm, wout_v.at[0]), (w_hbm, w_v), (keys_hbm, k_v), (values_hbm, v_v))):
        cp = pltpu.make_async_copy(src, dst, loc_sem.at[i])
        cp.start()
        fetches.append(cp)
    fetches[0].wait()

    rc = min(64, tok)
    p1s, p2s = [], []
    for r in range(tok // rc):
        p1 = jnp.zeros((rc, LANES), jnp.float32)
        p2 = jnp.zeros((rc, LANES), jnp.float32)
        for g in range(feat // LANES):
            xv = x_v[r * rc:(r + 1) * rc, g * LANES:(g + 1) * LANES].astype(jnp.float32)
            p1 = p1 + xv
            p2 = p2 + xv * xv
        p1s.append(p1)
        p2s.append(p2)
    if tok < tokp:
        p1s.append(jnp.zeros((tokp - tok, LANES), jnp.float32))
        p2s.append(jnp.zeros((tokp - tok, LANES), jnp.float32))
    s1 = jnp.sum(jnp.concatenate(p1s, axis=0).T, axis=0, keepdims=True)
    s2 = jnp.sum(jnp.concatenate(p2s, axis=0).T, axis=0, keepdims=True)
    stat_out[0:1, :] = s1
    stat_out[1:2, :] = s2
    stat_out[2:8, :] = jnp.zeros((6, tokp), jnp.float32)
    pl.semaphore_wait(barrier, T * K - 1)
    pending = []
    stat_copies = []
    for d in range(1, K):
        cp = pltpu.make_async_remote_copy(
            stat_out, stat_in.at[d - 1], st_s.at[d - 1], st_r.at[d - 1],
            device_id={"kv": kv_peer(d)}, device_id_type=MESH)
        cp.start()
        stat_copies.append(cp)
        pending.append(cp)
    fetches[1].wait()
    wo_copies = []
    for d in range(1, T):
        cp = pltpu.make_async_remote_copy(
            wout_v.at[0], wout_v.at[d], wo_s.at[d - 1], wo_r.at[d - 1],
            device_id={"tp": tp_peer(d)}, device_id_type=MESH)
        cp.start()
        wo_copies.append(cp)
        pending.append(cp)
    for cp in stat_copies:
        cp.wait_recv()
    for d in range(1, K):
        s1 = s1 + stat_in[d - 1, 0:1, :]
        s2 = s2 + stat_in[d - 1, 1:2, :]
    mean = s1 / D
    rstd = lax.rsqrt(s2 / D - mean * mean + epsilon)
    mean_c = jnp.broadcast_to(mean, (LANES, tokp)).T
    rstd_c = jnp.broadcast_to(rstd, (LANES, tokp)).T
    for r in range(tok // rc):
        mc = mean_c[r * rc:(r + 1) * rc]
        sc = rstd_c[r * rc:(r + 1) * rc]
        for g in range(feat // LANES):
            cols = slice(g * LANES, (g + 1) * LANES)
            xv = x_v[r * rc:(r + 1) * rc, cols].astype(jnp.float32)
            y = (xv - mc) * sc * params_ref[0:1, cols] + params_ref[1:2, cols]
            nrm[0, r * rc:(r + 1) * rc, cols] = y.astype(jnp.bfloat16)
    nm_copies = []
    for d in range(1, T):
        cp = pltpu.make_async_remote_copy(
            nrm.at[0], nrm.at[d], nm_s.at[d - 1], nm_r.at[d - 1],
            device_id={"tp": tp_peer(d)}, device_id_type=MESH)
        cp.start()
        nm_copies.append(cp)
        pending.append(cp)
    fetches[2].wait()

    rs_copies = []
    for d in range(T):
        if d:
            nm_copies[d - 1].wait_recv()
        part[d] = jnp.dot(nrm[d], w_v[...], preferred_element_type=jnp.float32)
        for i in range(tok // c):
            first = lax.rem(t - d + T, T) * tok + i * c
            owner = first // qb
            sub = lax.rem(first, qb) // c
            off = lax.rem(owner - z + K, K)
            slot = lax.rem(off + K - 1, K)
            cp = pltpu.make_async_remote_copy(
                part.at[d, pl.ds(i * c, c)], rbuf.at[slot, sub], rs_s.at[d * (tok // c) + i], rs_r.at[slot, sub],
                device_id={"kv": owner}, device_id_type=MESH)

            @pl.when(off != 0)
            def _():
                cp.start()

            @pl.when(off == 0)
            def _():
                rbuf[K - 1, sub] = part[d, i * c:(i + 1) * c]

            rs_copies.append((cp, off))
    fetches[3].wait()
    fetches[4].wait()
    vt_old = v_v[...].T
    for e in range(K - 1):
        for s in range(qb // c):
            pltpu.make_async_remote_copy(
                rbuf.at[e, s], rbuf.at[e, s], rs_s.at[0], rs_r.at[e, s],
                device_id={"kv": kv_peer(1)}, device_id_type=MESH).wait_recv()
    total = rbuf[K - 1]
    for e in range(K - 1):
        total = total + rbuf[e]
    proj = (total.reshape(qb, 3 * hd) + qkvb_ref[...]).astype(jnp.bfloat16)
    k_new = proj[:, hd:2 * hd]
    v_new = proj[:, 2 * hd:]
    q_buf[0] = proj[:, :hd]
    q_copies = []
    for d in range(1, K):
        cp = pltpu.make_async_remote_copy(
            q_buf.at[0], q_buf.at[d], q_s.at[d - 1], q_r.at[d - 1],
            device_id={"kv": kv_peer(d)}, device_id_type=MESH)
        cp.start()
        q_copies.append(cp)
        pending.append(cp)
    nk_ref[...] = k_new
    nv_ref[...] = v_new
    vt_new = v_new.T
    length = len_ref[0]
    scale = hd ** (-0.5)
    dims = (((1,), (1,)), ((), ()))
    old_seen = (z * part_len + lax.broadcasted_iota(jnp.int32, (part_len, qb), 0)) < length
    key_at = z * qb + lax.broadcasted_iota(jnp.int32, (qb, qb), 0)
    query_in = lax.broadcasted_iota(jnp.int32, (qb, qb), 1)

    def attend(d):
        q = q_buf[d]
        s_old = lax.dot_general(k_v[...], q, dims, preferred_element_type=jnp.float32) * scale
        s_new = lax.dot_general(k_new, q, dims, preferred_element_type=jnp.float32) * scale
        new_seen = key_at <= lax.rem(z - d + K, K) * qb + query_in
        s_old = jnp.where(old_seen, s_old, neg_large)
        s_new = jnp.where(new_seen, s_new, neg_large)
        m = jnp.maximum(jnp.max(s_old, axis=0, keepdims=True), jnp.max(s_new, axis=0, keepdims=True))
        w_old = jnp.where(old_seen, jnp.exp(s_old - m), 0.0)
        w_new = jnp.where(new_seen, jnp.exp(s_new - m), 0.0)
        l = jnp.sum(w_old, axis=0, keepdims=True) + jnp.sum(w_new, axis=0, keepdims=True)
        ot = jnp.dot(vt_old, w_old.astype(jnp.bfloat16), preferred_element_type=jnp.float32)
        ot = ot + jnp.dot(vt_new, w_new.astype(jnp.bfloat16), preferred_element_type=jnp.float32)
        return m, l, ot

    m0, l0, ot0 = attend(0)
    o_copies = []
    for d in range(1, K):
        q_copies[d - 1].wait_recv()
        m, l, ot = attend(d)
        ot_out[d - 1] = ot.astype(jnp.bfloat16)
        ml_out[d - 1, 0:1, :] = m
        ml_out[d - 1, 1:2, :] = l
        ml_out[d - 1, 2:8, :] = jnp.zeros((6, qb), jnp.float32)
        back = {"kv": kv_peer(K - d)}
        cpm = pltpu.make_async_remote_copy(
            ml_out.at[d - 1], ml_in.at[d - 1], m_s.at[d - 1], m_r.at[d - 1], device_id=back, device_id_type=MESH)
        cpm.start()
        cpo = pltpu.make_async_remote_copy(
            ot_out.at[d - 1], ot_in.at[d - 1], o_s.at[d - 1], o_r.at[d - 1], device_id=back, device_id_type=MESH)
        cpo.start()
        o_copies += [cpm, cpo]
        pending += [cpm, cpo]
    for cp in o_copies:
        cp.wait_recv()
    top = m0
    for d in range(1, K):
        top = jnp.maximum(top, ml_in[d - 1, 0:1, :])
    f = jnp.exp(m0 - top)
    l_all = l0 * f
    o_all = ot0 * f
    for d in range(1, K):
        f = jnp.exp(ml_in[d - 1, 0:1, :] - top)
        l_all = l_all + ml_in[d - 1, 1:2, :] * f
        o_all = o_all + ot_in[d - 1].astype(jnp.float32) * f
    att_own[...] = (o_all / l_all).T.astype(jnp.bfloat16)

    att_copies = []
    for s in range(qb // c):
        first = z * qb + s * c
        tp_own = first // tok
        slot = lax.rem(tp_own - t + T, T)
        at = lax.rem(first, tok) // c
        for e in list(range(1, K)) + [0]:
            cp = pltpu.make_async_remote_copy(
                att_own.at[pl.ds(s * c, c)], att_in.at[slot, at], a_s.at[s, e], a_r.at[slot, at],
                device_id={"tp": tp_own, "kv": kv_peer(e)}, device_id_type=MESH)
            if e:
                cp.start()
                att_copies.append((cp, None))
            else:
                @pl.when(slot != 0)
                def _():
                    cp.start()

                @pl.when(slot == 0)
                def _():
                    att_in[0, at] = att_own[s * c:(s + 1) * c]

                att_copies.append((cp, slot))
    for cp in wo_copies:
        cp.wait_recv()
    for d in range(T):
        for i in range(tok // c):
            def wait_in():
                pltpu.make_async_remote_copy(
                    att_in.at[d, i], att_in.at[d, i], a_s.at[0, 0], a_r.at[d, i],
                    device_id={"kv": kv_peer(1)}, device_id_type=MESH).wait_recv()
            if d:
                wait_in()
            else:
                pl.when((t * tok + i * c) // qb != z)(wait_in)
    att = jnp.concatenate([att_in[d].reshape(tok, hd) for d in range(T)], axis=1)
    wide = 256 if feat % 256 == 0 else feat
    for g in range(feat // wide):
        cols = slice(g * wide, (g + 1) * wide)
        w = jnp.concatenate([wout_v[d, :, cols] for d in range(T)], axis=0)
        y = jnp.dot(att, w, preferred_element_type=jnp.float32)
        y = y + params_ref[2:3, cols] + x_v[:, cols].astype(jnp.float32)
        out_ref[:, cols] = y.astype(jnp.bfloat16)

    for cp in pending:
        cp.wait_send()
    for cp, off in rs_copies:
        pl.when(off != 0)(cp.wait_send)
    for cp, slot in att_copies:
        if slot is None:
            cp.wait_send()
        else:
            pl.when(slot != 0)(cp.wait_send)


def on_device(T, K, hidden_in, lengths, ln_gain, ln_bias, w_qkv, qkv_bias, cache_keys, cache_values, w_out, out_bias):
    _, tok, feat = hidden_in.shape
    hd = cache_keys.shape[3]
    part_len = cache_keys.shape[2]
    group = T * tok
    qb = group // K
    c = min(tok, qb)
    tokp = max(tok, LANES)
    params = jnp.stack([ln_gain, ln_bias, out_bias]).astype(jnp.float32)
    qkvb = qkv_bias.astype(jnp.float32)[None]
    bf, f32 = jnp.bfloat16, jnp.float32
    dma = pltpu.SemaphoreType.DMA
    any_spec = pl.BlockSpec(memory_space=pl.ANY)
    vm = pl.BlockSpec(memory_space=pltpu.VMEM)
    n1 = max(T - 1, 1)
    out, nk, nv = pl.pallas_call(
        functools.partial(kernel, T, K, feat * K),
        out_shape=(
            jax.ShapeDtypeStruct((tok, feat), bf),
            jax.ShapeDtypeStruct((qb, hd), bf),
            jax.ShapeDtypeStruct((qb, hd), bf),
        ),
        in_specs=[pl.BlockSpec(memory_space=pltpu.SMEM)] + [any_spec] * 5 + [vm, vm],
        out_specs=(vm, vm, vm),
        scratch_shapes=[
            pltpu.VMEM((tok, feat), bf),
            pltpu.VMEM((feat, 3 * hd), bf),
            pltpu.VMEM((part_len, hd), bf),
            pltpu.VMEM((part_len, hd), bf),
            pltpu.VMEM((T, hd, feat), bf),
            pltpu.VMEM((8, tokp), f32),
            pltpu.VMEM((K - 1, 8, tokp), f32),
            pltpu.VMEM((T, tok, feat), bf),
            pltpu.VMEM((T, tok, 3 * hd), f32),
            pltpu.VMEM((K, qb // c, c, 3 * hd), f32),
            pltpu.VMEM((K, qb, hd), bf),
            pltpu.VMEM((K - 1, hd, qb), bf),
            pltpu.VMEM((K - 1, hd, qb), bf),
            pltpu.VMEM((K - 1, 8, qb), f32),
            pltpu.VMEM((K - 1, 8, qb), f32),
            pltpu.VMEM((qb, hd), bf),
            pltpu.VMEM((T, tok // c, c, hd), bf),
            dma((5,)),
            dma((K - 1,)), dma((K - 1,)),
            dma((n1,)), dma((n1,)),
            dma((n1,)), dma((n1,)),
            dma((T * (tok // c),)), dma((K - 1, qb // c)),
            dma((K - 1,)), dma((K - 1,)),
            dma((K - 1,)), dma((K - 1,)),
            dma((K - 1,)), dma((K - 1,)),
            dma((qb // c, K)), dma((T, tok // c)),
        ],
        compiler_params=pltpu.CompilerParams(
            collective_id=0, has_side_effects=True, vmem_limit_bytes=48 * 1024 * 1024),
    )(lengths, hidden_in[0], w_qkv, cache_keys[0, 0], cache_values[0, 0], w_out, params, qkvb)
    return out[None], nk[None, None], nv[None, None]


def solution(mesh):
    placed = (
        P("req", "tp", "kv"),
        P("req"),
        P("kv"),
        P("kv"),
        P("kv", "tp"),
        P("tp"),
        P("req", "tp", "kv", None),
        P("req", "tp", "kv", None),
        P("tp", "kv"),
        P("kv"),
    )
    return jax.shard_map(
        functools.partial(on_device, mesh.shape["tp"], mesh.shape["kv"]),
        mesh=mesh,
        in_specs=placed,
        out_specs=(P("req", "tp", "kv"), P("req", "tp", "kv", None), P("req", "tp", "kv", None)),
        check_vma=False,
    )
```

time: 151 us -> 52.8 us (0.35)
  waiting for transfers between devices: 90.7 us -> 0 us
  Pallas kernels: 0 us -> 40.9 us
  blocking collectives: 25.8 us -> 0 us
  between operations: 14.6 us -> 1.3 us
  matrix products: 9.28 us -> 0 us
  local copies, waits for them, and re-layouts: 1.61 us -> 10.2 us
  other arithmetic: 8.2 us -> 0.03 us
    psum x2 -> x0, waiting for transfers between devices: 69.5 us -> none  [the longest x1 43.8 us: on_device(): summed = lax.psum(partial_value, 'kv')]
    pallas_call x0 -> x1, Pallas kernels: none -> 40.9 us  [on_device(): pl.pallas_call(functools.partial(kernel, T, K, feat * K), out_shape=(jax....]
    psum x2 -> x0, blocking collectives: 17.9 us -> none  [the longest x1 10.8 us: on_device(): lax.psum((jnp.sum(rows, axis=1), jnp.sum(rows * rows, axis=1)), 'kv')]
    all_gather x1 -> x0, waiting for transfers between devices: 10.9 us -> none  [on_device(): lax.all_gather(normed, 'tp', axis=0, tiled=True)]
    reduce_scatter x1 -> x0, waiting for transfers between devices: 10.2 us -> none  [on_device(): lax.psum_scatter(jnp.dot(attended, w_out, preferred_element_type=jnp.floa...]
    dot_general x6 -> x0, matrix products: 9.28 us -> none  [the longest x1 3.49 us: on_device(): jnp.dot(lax.all_gather(normed, 'tp', axis=0, tiled=True), w_qkv, preferre...]
    pmax x1 -> x0, blocking collectives: 7.82 us -> none  [on_device(): global_max = lax.pmax(row_max, 'kv')]
    unnamed x16 -> x13, local copies, waits for them, and re-layouts: 0.19 us -> 7.47 us
  transfers between devices with their start and end apart: 4 -> 0, of which waited for: 4 -> 0; matrix products, arithmetic and copies ran while one was open for 1% -> 0% of each run, Pallas kernels for 0% -> 0%
where the time goes in v1:
time: 52.8 us; the launch traced here: 52.4 us
  Pallas kernels  40.9 us (77%)
  local copies, waits for them, and re-layouts  10.2 us (19%)
  between operations  1.3 us (2%)
    pallas_call x1, Pallas kernels, on_device(): pl.pallas_call(functools.partial(kernel, T, K, feat * K), out_shape=(jax....  40.9 us
    unnamed x13, local copies, waits for them, and re-layouts  7.47 us
    another operation x3, local copies, waits for them, and re-layouts, on_device(): params = jnp.stack([ln_gain, ln_bias, out_bias]).astype(jnp.float32)  2.08 us

profile of v1, /device:TPU:1, one launch (start us, length us, event | category | flops | bytes accessed | tf_op | source)
XLA Modules:
  0.0 52.4 jit_solution(15655205925569515806)
XLA Ops:
  1.3 0.7 %reshape.6.qkvb_ref = f32[1,384]{1,0:T(1,128)S(1)} reshape(bf16[384]{0:T(512)(128)(2,1)} %param.15) | data formatting | bytes 2304 | tf_op jit(solution)/shard_map/broadcast_in_dim | solution.py:285
  2.0 0.7 %stack.12 = bf16[1,1792]{1,0:T(2,128)(2,1)S(1)} reshape(bf16[1792]{0:T(1024)(128)(2,1)} %param.12) | data formatting | bytes 7168 | tf_op jit(solution)/shard_map/stack | solution.py:284
  2.7 0.7 %stack.13 = bf16[1,1792]{1,0:T(2,128)(2,1)S(1)} reshape(bf16[1792]{0:T(1024)(128)(2,1)} %param.13) | data formatting | bytes 7168 | tf_op jit(solution)/shard_map/stack | solution.py:284
  3.3 0.7 %stack.14 = bf16[1,1792]{1,0:T(2,128)(2,1)S(1)} reshape(bf16[1792]{0:T(1024)(128)(2,1)} %param.19) | data formatting | bytes 7168 | tf_op jit(solution)/shard_map/stack | solution.py:284
  4.1 0.0 copy-start
  4.1 1.3 %copy-done = bf16[1792,384]{1,0:T(8,128)(2,1)S(1)} copy-done((bf16[1792,384]{1,0:T(8,128)(2,1)S(1)}, bf16[1792,384]{1,0:T(8,128)(2,1)}, u32[]{:S(2)}) %copy-start) | copy-done | bytes 1376280
  5.4 0.0 copy-start.1
  5.4 1.2 %copy-done.1 = bf16[1,256,1792]{2,1,0:T(8,128)(2,1)S(1)} copy-done((bf16[1,256,1792]{2,1,0:T(8,128)(2,1)S(1)}, bf16[1,256,1792]{2,1,0:T(8,128)(2,1)}, u32[]{:S(2)}) %copy-start.1) | copy-done | bytes 917528
  6.6 0.0 copy-start.2
  6.6 1.0 %copy-done.2 = bf16[128,1792]{1,0:T(8,128)(2,1)S(1)} copy-done((bf16[128,1792]{1,0:T(8,128)(2,1)S(1)}, bf16[128,1792]{1,0:T(8,128)(2,1)}, u32[]{:S(2)}) %copy-start.2) | copy-done | bytes 458776
  7.6 0.0 copy-start.3
  7.6 0.9 %copy-done.3 = bf16[1,1,384,128]{3,2,1,0:T(8,128)(2,1)S(1)} copy-done((bf16[1,1,384,128]{3,2,1,0:T(8,128)(2,1)S(1)}, bf16[1,1,384,128]{3,2,1,0:T(8,128)(2,1)}, u32[]{:S(2)}) %copy-start.3) | copy-done | bytes 98328
  8.5 0.0 copy-start.4
  8.5 0.9 %copy-done.4 = bf16[1,1,384,128]{3,2,1,0:T(8,128)(2,1)S(1)} copy-done((bf16[1,1,384,128]{3,2,1,0:T(8,128)(2,1)S(1)}, bf16[1,1,384,128]{3,2,1,0:T(8,128)(2,1)}, u32[]{:S(2)}) %copy-start.4) | copy-done | bytes 98328
  9.4 40.9 %shard_map.121 = (bf16[256,1792]{1,0:T(8,128)(2,1)S(1)}, bf16[128,128]{1,0:T(8,128)(2,1)S(1)}, bf16[128,128]{1,0:T(8,128)(2,1)S(1)}) custom-call(s32[1]{0:T(128)S(6)} %copy.16.len_ref, bf16[256,1792]{1,0:T(8,128)(2,1)S(1)} %bitcast.7, bf16[1792,384]{1,0:T(8,128)(2,1)S(1)} %copy-done, bf16[384,128]{1,0:T(8,128)(2,1)S(1)} %bitcast.8, ...), custom_call_target="tpu_custom_call" | custom-call | tf_op jit(solution)/shard_map/pallas_call | solution.py:291
  50.3 0.9 %copy.17 = bf16[1,256,1792]{2,1,0:T(8,128)(2,1)} copy(bf16[1,256,1792]{2,1,0:T(8,128)(2,1)S(1)} %bitcast.6) | data formatting | bytes 1835008
  51.2 0.6 %copy.18 = bf16[1,1,128,128]{3,2,1,0:T(8,128)(2,1)} copy(bf16[1,1,128,128]{3,2,1,0:T(8,128)(2,1)S(1)} %bitcast.11) | data formatting | bytes 65536
  51.8 0.6 %copy.19 = bf16[1,1,128,128]{3,2,1,0:T(8,128)(2,1)} copy(bf16[1,1,128,128]{3,2,1,0:T(8,128)(2,1)S(1)} %bitcast.10) | data formatting | bytes 65536
  (1 shorter events, 0.0 us)
Async XLA Ops:
  4.1 1.3 %copy-start = (bf16[1792,384]{1,0:T(8,128)(2,1)S(1)}, bf16[1792,384]{1,0:T(8,128)(2,1)}, u32[]{:S(2)}) copy-start(bf16[1792,384]{1,0:T(8,128)(2,1)} %w_hbm.1) | copy-start | bytes 4128772
  5.4 1.2 %copy-start.1 = (bf16[1,256,1792]{2,1,0:T(8,128)(2,1)S(1)}, bf16[1,256,1792]{2,1,0:T(8,128)(2,1)}, u32[]{:S(2)}) copy-start(bf16[1,256,1792]{2,1,0:T(8,128)(2,1)} %param.10) | copy-start | bytes 2752516
  6.6 1.0 %copy-start.2 = (bf16[128,1792]{1,0:T(8,128)(2,1)S(1)}, bf16[128,1792]{1,0:T(8,128)(2,1)}, u32[]{:S(2)}) copy-start(bf16[128,1792]{1,0:T(8,128)(2,1)} %wout_hbm.1) | copy-start | bytes 1376260
  7.6 0.9 %copy-start.3 = (bf16[1,1,384,128]{3,2,1,0:T(8,128)(2,1)S(1)}, bf16[1,1,384,128]{3,2,1,0:T(8,128)(2,1)}, u32[]{:S(2)}) copy-start(bf16[1,1,384,128]{3,2,1,0:T(8,128)(2,1)} %param.16) | copy-start | bytes 294916
  8.5 0.9 %copy-start.4 = (bf16[1,1,384,128]{3,2,1,0:T(8,128)(2,1)S(1)}, bf16[1,1,384,128]{3,2,1,0:T(8,128)(2,1)}, u32[]{:S(2)}) copy-start(bf16[1,1,384,128]{3,2,1,0:T(8,128)(2,1)} %param.17) | copy-start | bytes 294916

commit v2 on v1

--- a/solution.py
+++ b/solution.py
@@ -15,11 +15,11 @@
 
 def kernel(
     T, K, D,
-    len_ref, x_hbm, w_hbm, keys_hbm, values_hbm, wout_hbm, params_ref, qkvb_ref,
+    len_ref, x_hbm, w_hbm, keys_hbm, values_hbm, wout_hbm, gain_ref, lnb_ref, outb_ref, qkvb_ref,
     out_ref, nk_ref, nv_ref,
     x_v, w_v, k_v, v_v, wout_v,
-    stat_out, stat_in, nrm, part, rbuf, q_buf, ot_out, ot_in, ml_out, ml_in, att_own, att_in,
-    loc_sem, st_s, st_r, nm_s, nm_r, wo_s, wo_r, rs_s, rs_r, q_s, q_r, o_s, o_r, m_s, m_r, a_s, a_r,
+    stat_out, stat_in, nrm, part_q, part_kv, rbuf_q, rbuf_kv, q_buf, ot_out, ot_in, ml_out, ml_in, att_own, att_in,
+    loc_sem, st_s, st_r, nm_s, nm_r, wo_s, wo_r, rq_s, rq_r, rkv_s, rkv_r, q_s, q_r, o_s, o_r, m_s, m_r, a_s, a_r,
 ):
     t = lax.axis_index("tp")
     z = lax.axis_index("kv")
@@ -36,6 +36,9 @@
 
     def tp_peer(d):
         return lax.rem(t + d, T)
+
+    def row(ref):
+        return ref[...].astype(jnp.float32).reshape(1, ref.shape[0])
 
     barrier = pltpu.get_barrier_semaphore()
     for a in range(T):
@@ -92,6 +95,8 @@
     for d in range(1, K):
         s1 = s1 + stat_in[d - 1, 0:1, :]
         s2 = s2 + stat_in[d - 1, 1:2, :]
+    gain = row(gain_ref)
+    shift = row(lnb_ref)
     mean = s1 / D
     rstd = lax.rsqrt(s2 / D - mean * mean + epsilon)
     mean_c = jnp.broadcast_to(mean, (LANES, tokp)).T
@@ -102,7 +107,7 @@
         for g in range(feat // LANES):
             cols = slice(g * LANES, (g + 1) * LANES)
             xv = x_v[r * rc:(r + 1) * rc, cols].astype(jnp.float32)
-            y = (xv - mc) * sc * params_ref[0:1, cols] + params_ref[1:2, cols]
+            y = (xv - mc) * sc * gain[:, cols] + shift[:, cols]
             nrm[0, r * rc:(r + 1) * rc, cols] = y.astype(jnp.bfloat16)
     nm_copies = []
     for d in range(1, T):
@@ -115,10 +120,8 @@
     fetches[2].wait()
 
     rs_copies = []
-    for d in range(T):
-        if d:
-            nm_copies[d - 1].wait_recv()
-        part[d] = jnp.dot(nrm[d], w_v[...], preferred_element_type=jnp.float32)
+
+    def scatter(d, part, rbuf, s_sem, r_sem):
         for i in range(tok // c):
             first = lax.rem(t - d + T, T) * tok + i * c
             owner = first // qb
@@ -126,7 +129,7 @@
             off = lax.rem(owner - z + K, K)
             slot = lax.rem(off + K - 1, K)
             cp = pltpu.make_async_remote_copy(
-                part.at[d, pl.ds(i * c, c)], rbuf.at[slot, sub], rs_s.at[d * (tok // c) + i], rs_r.at[slot, sub],
+                part.at[d, pl.ds(i * c, c)], rbuf.at[slot, sub], s_sem.at[d * (tok // c) + i], r_sem.at[slot, sub],
                 device_id={"kv": owner}, device_id_type=MESH)
 
             @pl.when(off != 0)
@@ -138,21 +141,37 @@
                 rbuf[K - 1, sub] = part[d, i * c:(i + 1) * c]
 
             rs_copies.append((cp, off))
+
+    def gathered(rbuf, s_sem, r_sem, bias):
+        for e in range(K - 1):
+            for s in range(qb // c):
+                pltpu.make_async_remote_copy(
+                    rbuf.at[e, s], rbuf.at[e, s], s_sem.at[0], r_sem.at[e, s],
+                    device_id={"kv": kv_peer(1)}, device_id_type=MESH).wait_recv()
+        total = rbuf[K - 1]
+        for e in range(K - 1):
+            total = total + rbuf[e]
+        return (total.reshape(qb, rbuf.shape[3]) + bias).astype(jnp.bfloat16)
+
+    def project(d, lo, hi, part):
+        part[d] = jnp.dot(nrm[d], w_v[:, lo:hi], preferred_element_type=jnp.float32)
+
+    project(0, 0, hd, part_q)
+    scatter(0, part_q, rbuf_q, rq_s, rq_r)
+    project(0, hd, 3 * hd, part_kv)
+    for d in range(1, T):
+        nm_copies[d - 1].wait_recv()
+        project(d, 0, hd, part_q)
+        scatter(d, part_q, rbuf_q, rq_s, rq_r)
+    scatter(0, part_kv, rbuf_kv, rkv_s, rkv_r)
+    for d in range(1, T):
+        project(d, hd, 3 * hd, part_kv)
+        scatter(d, part_kv, rbuf_kv, rkv_s, rkv_r)
     fetches[3].wait()
     fetches[4].wait()
     vt_old = v_v[...].T
-    for e in range(K - 1):
-        for s in range(qb // c):
-            pltpu.make_async_remote_copy(
-                rbuf.at[e, s], rbuf.at[e, s], rs_s.at[0], rs_r.at[e, s],
-                device_id={"kv": kv_peer(1)}, device_id_type=MESH).wait_recv()
-    total = rbuf[K - 1]
-    for e in range(K - 1):
-        total = total + rbuf[e]
-    proj = (total.reshape(qb, 3 * hd) + qkvb_ref[...]).astype(jnp.bfloat16)
-    k_new = proj[:, hd:2 * hd]
-    v_new = proj[:, 2 * hd:]
-    q_buf[0] = proj[:, :hd]
+    qkv_bias = row(qkvb_ref)
+    q_buf[0] = gathered(rbuf_q, rq_s, rq_r, qkv_bias[:, :hd])
     q_copies = []
     for d in range(1, K):
         cp = pltpu.make_async_remote_copy(
@@ -161,9 +180,6 @@
         cp.start()
         q_copies.append(cp)
         pending.append(cp)
-    nk_ref[...] = k_new
-    nv_ref[...] = v_new
-    vt_new = v_new.T
     length = len_ref[0]
     scale = hd ** (-0.5)
     dims = (((1,), (1,)), ((), ()))
@@ -171,25 +187,35 @@
     key_at = z * qb + lax.broadcasted_iota(jnp.int32, (qb, qb), 0)
     query_in = lax.broadcasted_iota(jnp.int32, (qb, qb), 1)
 
+    def weigh(keys, q, seen, vt):
+        s = lax.dot_general(keys, q, dims, preferred_element_type=jnp.float32) * scale
+        s = jnp.where(seen, s, neg_large)
+        m = jnp.max(s, axis=0, keepdims=True)
+        w = jnp.where(seen, jnp.exp(s - m), 0.0)
+        l = jnp.sum(w, axis=0, keepdims=True)
+        return m, l, jnp.dot(vt, w.astype(jnp.bfloat16), preferred_element_type=jnp.float32)
+
+    olds = []
+    for d in range(K):
+        if d:
+            q_copies[d - 1].wait_recv()
+        olds.append(weigh(k_v[...], q_buf[d], old_seen, vt_old))
+    kv_new = gathered(rbuf_kv, rkv_s, rkv_r, qkv_bias[:, hd:])
+    k_new = kv_new[:, :hd]
+    v_new = kv_new[:, hd:]
+    vt_new = v_new.T
+
     def attend(d):
-        q = q_buf[d]
-        s_old = lax.dot_general(k_v[...], q, dims, preferred_element_type=jnp.float32) * scale
-        s_new = lax.dot_general(k_new, q, dims, preferred_element_type=jnp.float32) * scale
+        m_old, l_old, ot_old = olds[d]
         new_seen = key_at <= lax.rem(z - d + K, K) * qb + query_in
-        s_old = jnp.where(old_seen, s_old, neg_large)
-        s_new = jnp.where(new_seen, s_new, neg_large)
-        m = jnp.maximum(jnp.max(s_old, axis=0, keepdims=True), jnp.max(s_new, axis=0, keepdims=True))
-        w_old = jnp.where(old_seen, jnp.exp(s_old - m), 0.0)
-        w_new = jnp.where(new_seen, jnp.exp(s_new - m), 0.0)
-        l = jnp.sum(w_old, axis=0, keepdims=True) + jnp.sum(w_new, axis=0, keepdims=True)
-        ot = jnp.dot(vt_old, w_old.astype(jnp.bfloat16), preferred_element_type=jnp.float32)
-        ot = ot + jnp.dot(vt_new, w_new.astype(jnp.bfloat16), preferred_element_type=jnp.float32)
-        return m, l, ot
-
-    m0, l0, ot0 = attend(0)
+        m_new, l_new, ot_new = weigh(k_new, q_buf[d], new_seen, vt_new)
+        m = jnp.maximum(m_old, m_new)
+        f_old = jnp.exp(m_old - m)
+        f_new = jnp.exp(m_new - m)
+        return m, l_old * f_old + l_new * f_new, ot_old * f_old + ot_new * f_new
+
     o_copies = []
     for d in range(1, K):
-        q_copies[d - 1].wait_recv()
         m, l, ot = attend(d)
         ot_out[d - 1] = ot.astype(jnp.bfloat16)
         ml_out[d - 1, 0:1, :] = m
@@ -204,6 +230,9 @@
         cpo.start()
         o_copies += [cpm, cpo]
         pending += [cpm, cpo]
+    nk_ref[...] = k_new
+    nv_ref[...] = v_new
+    m0, l0, ot0 = attend(0)
     for cp in o_copies:
         cp.wait_recv()
     top = m0
@@ -254,12 +283,13 @@
             else:
                 pl.when((t * tok + i * c) // qb != z)(wait_in)
     att = jnp.concatenate([att_in[d].reshape(tok, hd) for d in range(T)], axis=1)
+    out_bias = row(outb_ref)
     wide = 256 if feat % 256 == 0 else feat
     for g in range(feat // wide):
         cols = slice(g * wide, (g + 1) * wide)
         w = jnp.concatenate([wout_v[d, :, cols] for d in range(T)], axis=0)
         y = jnp.dot(att, w, preferred_element_type=jnp.float32)
-        y = y + params_ref[2:3, cols] + x_v[:, cols].astype(jnp.float32)
+        y = y + out_bias[:, cols] + x_v[:, cols].astype(jnp.float32)
         out_ref[:, cols] = y.astype(jnp.bfloat16)
 
     for cp in pending:
@@ -273,6 +303,17 @@
             pl.when(slot != 0)(cp.wait_send)
 
 
+def place(a_ref, b_ref, c_ref, a_out, b_out, c_out, sem):
+    copies = [
+        pltpu.make_async_copy(src, dst, sem.at[i])
+        for i, (src, dst) in enumerate(((a_ref, a_out), (b_ref, b_out), (c_ref, c_out)))
+    ]
+    for cp in copies:
+        cp.start()
+    for cp in copies:
+        cp.wait()
+
+
 def on_device(T, K, hidden_in, lengths, ln_gain, ln_bias, w_qkv, qkv_bias, cache_keys, cache_values, w_out, out_bias):
     _, tok, feat = hidden_in.shape
     hd = cache_keys.shape[3]
@@ -281,11 +322,9 @@
     qb = group // K
     c = min(tok, qb)
     tokp = max(tok, LANES)
-    params = jnp.stack([ln_gain, ln_bias, out_bias]).astype(jnp.float32)
-    qkvb = qkv_bias.astype(jnp.float32)[None]
     bf, f32 = jnp.bfloat16, jnp.float32
     dma = pltpu.SemaphoreType.DMA
-    any_spec = pl.BlockSpec(memory_space=pl.ANY)
+    any_spec = pl.BlockSpec(memory_space=pltpu.HBM)
     vm = pl.BlockSpec(memory_space=pltpu.VMEM)
     n1 = max(T - 1, 1)
     out, nk, nv = pl.pallas_call(
@@ -295,7 +334,7 @@
             jax.ShapeDtypeStruct((qb, hd), bf),
             jax.ShapeDtypeStruct((qb, hd), bf),
         ),
-        in_specs=[pl.BlockSpec(memory_space=pltpu.SMEM)] + [any_spec] * 5 + [vm, vm],
+        in_specs=[pl.BlockSpec(memory_space=pltpu.SMEM)] + [any_spec] * 5 + [vm] * 4,
         out_specs=(vm, vm, vm),
         scratch_shapes=[
             pltpu.VMEM((tok, feat), bf),
@@ -306,8 +345,10 @@
             pltpu.VMEM((8, tokp), f32),
             pltpu.VMEM((K - 1, 8, tokp), f32),
             pltpu.VMEM((T, tok, feat), bf),
-            pltpu.VMEM((T, tok, 3 * hd), f32),
-            pltpu.VMEM((K, qb // c, c, 3 * hd), f32),
+            pltpu.VMEM((T, tok, hd), f32),
+            pltpu.VMEM((T, tok, 2 * hd), f32),
+            pltpu.VMEM((K, qb // c, c, hd), f32),
+            pltpu.VMEM((K, qb // c, c, 2 * hd), f32),
             pltpu.VMEM((K, qb, hd), bf),
             pltpu.VMEM((K - 1, hd, qb), bf),
             pltpu.VMEM((K - 1, hd, qb), bf),
@@ -320,14 +361,23 @@
             dma((n1,)), dma((n1,)),
             dma((n1,)), dma((n1,)),
             dma((T * (tok // c),)), dma((K - 1, qb // c)),
+            dma((T * (tok // c),)), dma((K - 1, qb // c)),
             dma((K - 1,)), dma((K - 1,)),
             dma((K - 1,)), dma((K - 1,)),
             dma((K - 1,)), dma((K - 1,)),
             dma((qb // c, K)), dma((T, tok // c)),
         ],
         compiler_params=pltpu.CompilerParams(
-            collective_id=0, has_side_effects=True, vmem_limit_bytes=48 * 1024 * 1024),
-    )(lengths, hidden_in[0], w_qkv, cache_keys[0, 0], cache_values[0, 0], w_out, params, qkvb)
+            collective_id=0, has_side_effects=True),
+    )(lengths, hidden_in[0], w_qkv, cache_keys[0, 0], cache_values[0, 0], w_out, ln_gain, ln_bias, out_bias, qkv_bias)
+    held = [pl.BlockSpec(memory_space=pl.ANY)] * 3
+    out, nk, nv = pl.pallas_call(
+        place,
+        out_shape=tuple(jax.ShapeDtypeStruct(a.shape, a.dtype) for a in (out, nk, nv)),
+        in_specs=held,
+        out_specs=tuple(held),
+        scratch_shapes=[dma((3,))],
+    )(out, nk, nv)
     return out[None], nk[None, None], nv[None, None]
 
 

time: 52.8 us -> 76.1 us (1.44)
  Pallas kernels: 40.9 us -> 74.6 us
  local copies, waits for them, and re-layouts: 10.2 us -> 0 us
    pallas_call x0 -> x1, Pallas kernels: none -> 30.9 us  [on_device(): pl.pallas_call(place, out_shape=tuple((jax.ShapeDtypeStruct(a.shape, a.dt...]
    unnamed x13 -> x0, local copies, waits for them, and re-layouts: 7.47 us -> none
    pallas_call x1, Pallas kernels: 40.9 us -> 43.7 us  [on_device(): pl.pallas_call(functools.partial(kernel, T, K, feat * K), out_shape=(jax....]
    another operation x3 -> x0, local copies, waits for them, and re-layouts: 2.08 us -> none  [on_device(): params = jnp.stack([ln_gain, ln_bias, out_bias]).astype(jnp.float32)]
where the time goes in v2:
time: 76.1 us; the launch traced here: 75.9 us
  Pallas kernels  74.6 us (98%)
  between operations  1.29 us (2%)
    pallas_call x1, Pallas kernels, on_device(): pl.pallas_call(functools.partial(kernel, T, K, feat * K), out_shape=(jax....  43.7 us
    pallas_call x1, Pallas kernels, on_device(): pl.pallas_call(place, out_shape=tuple((jax.ShapeDtypeStruct(a.shape, a.dt...  30.9 us

profile of v2, /device:TPU:1, one launch (start us, length us, event | category | flops | bytes accessed | tf_op | source)
XLA Modules:
  0.0 75.9 jit_solution(14675095530516057774)
XLA Ops:
  1.3 43.7 %shard_map.121 = (bf16[256,1792]{1,0:T(8,128)(2,1)}, bf16[128,128]{1,0:T(8,128)(2,1)}, bf16[128,128]{1,0:T(8,128)(2,1)}) custom-call(s32[1]{0:T(128)S(6)} %copy.13.len_ref, bf16[256,1792]{1,0:T(8,128)(2,1)} %bitcast.6, bf16[1792,384]{1,0:T(8,128)(2,1)} %w_hbm.1, bf16[384,128]{1,0:T(8,128)(2,1)} %bitcast.7, bf16[384,128]{1,0:T(8,128)(2,1)} %bitcast.8, ...), custom_call_target="tpu_custom_call" | custom-call | tf_op jit(solution)/shard_map/pallas_call | solution.py:330
  45.0 30.9 %shard_map.122 = (bf16[256,1792]{1,0:T(8,128)(2,1)}, bf16[128,128]{1,0:T(8,128)(2,1)}, bf16[128,128]{1,0:T(8,128)(2,1)}) custom-call(bf16[256,1792]{1,0:T(8,128)(2,1)} %get-tuple-element.9.a_ref, bf16[128,128]{1,0:T(8,128)(2,1)} %get-tuple-element.10.b_ref, bf16[128,128]{1,0:T(8,128)(2,1)} %get-tuple-element.11.c_ref), custom_call_target="tpu_custom_call" | custom-call | tf_op jit(solution)/shard_map/pallas_call | solution.py:374
